TPU v7x, 512 devices: a whole 4x4x16 slice. The times are simulated.
512 devices in a mesh: wide: 128 (over z, x, core), narrow: 4 (over y).
Axes of the slice: x: 4, y: 4, z: 16, core: 2. Of those that a mesh axis runs over, the one named last changes fastest.
Arguments:
- tokens_in: bfloat16 [16384, 2560], P('wide', 'narrow'), may hold values from -6 to 6
- norm_gain: bfloat16 [2560], replicated, may hold values from 0.099609375 to 1.8984375
- query_weight: bfloat16 [2560, 2560], P('wide', 'narrow'), may hold values from -0.25 to 0.25
- key_weight: bfloat16 [2560, 640], P('wide', 'narrow'), may hold values from -0.125 to 0.125
- value_weight: bfloat16 [2560, 640], P('wide', 'narrow'), may hold values from -0.5 to 0.5
- out_weight: bfloat16 [2560, 2560], P('wide', 'narrow'), may hold values from -0.125 to 0.125
- cache_keys: bfloat16 [640, 131072], P('narrow', 'wide'), may hold values from -64 to 64
- cache_values: bfloat16 [640, 131072], P('narrow', 'wide'), may hold values from -24 to 24
- cached_len: int32 [32], replicated, may hold values from 1 to 4096, as said below
- append_slot: int32 [32], replicated, may hold values from 0 to 4095
- shard_owner: int32 [32], replicated, may hold values from 0 to 3
Outputs:
- attention_update: bfloat16 [16384, 2560], P('wide', 'narrow')
- appended_keys: bfloat16 [640, 131072], P('narrow', 'wide')
- appended_values: bfloat16 [640, 131072], P('narrow', 'wide')
Inputs may be any that keep to these rules, and one draw needn't show every extreme that they name: `cached_len`: each request's number of cached keys; some request holds 4096.
All inputs are finite; a program needn't handle non-finite values.
Results may differ from a plain program's by a relative error of at most 0.012.
The roundings to bfloat16 on the way count: a program that leaves them out, or rounds other values in their place, can miss the bound.
Values may be sent and summed in bfloat16 or wider, within the bound.
A program may use at most 64 MiB of HBM per device.

v0:
```python
import math
import jax
import jax.numpy as jnp
from jax import lax
from jax.sharding import PartitionSpec as P

HEAD_DIM = 80
WIN = 4096
GROUP_BITS = 2
GROUP = 4
EPSILON = 1e-05
ROPE_BASE = 10000.0
LOWEST = -1e30


def from_partner(block, axis, bit):
    count = lax.axis_size(axis)
    route = []
    for low in range(count):
        high = low | 1 << bit
        if high != low and high < count:
            route += [(low, high), (high, low)]
    return lax.ppermute(block, axis, route)


def rms_normed(rows_in, gain):
    values = rows_in.astype(jnp.float32)
    scaling = lax.rsqrt(jnp.mean(values * values, axis=-1, keepdims=True) + EPSILON)
    return (values * scaling * gain.astype(jnp.float32)).astype(jnp.bfloat16)


def rotate(values, positions):
    half_dim = values.shape[-1] // 2
    inverse = ROPE_BASE ** (-(jnp.arange(half_dim, dtype=jnp.float32) * (2.0 / values.shape[-1])))
    angles = positions.astype(jnp.float32)[:, None] * inverse[None, :]
    cos_part = jnp.cos(angles)[:, None, :]
    sin_part = jnp.sin(angles)[:, None, :]
    lower = values[..., :half_dim]
    higher = values[..., half_dim:]
    return jnp.concatenate(
        [lower * cos_part - higher * sin_part, higher * cos_part + lower * sin_part], axis=-1
    )


def ordered(mine, other, upper, along):
    first_half = jnp.where(upper, other, mine)
    second_half = jnp.where(upper, mine, other)
    return jnp.concatenate([first_half, second_half], axis=along)


def empty_state(row_count, groups, repeats):
    return (
        jnp.zeros((row_count, groups, repeats, HEAD_DIM), jnp.float32),
        jnp.full((row_count, groups, repeats), LOWEST, jnp.float32),
        jnp.zeros((row_count, groups, repeats), jnp.float32),
    )


def fold_keys(state, queries, query_pos, keys, values, key_pos, key_ok, widest):
    key_count = keys.shape[1]
    groups = queries.shape[1]
    block = math.gcd(key_count, widest)
    keys_split = keys.reshape(groups, HEAD_DIM, key_count)
    values_split = values.reshape(groups, HEAD_DIM, key_count)
    scale = HEAD_DIM ** (-0.5)

    def step(index, carry):
        accum, top_old, sum_old = carry
        start = index * block
        block_keys = lax.dynamic_slice_in_dim(keys_split, start, block, 2)
        block_values = lax.dynamic_slice_in_dim(values_split, start, block, 2)
        block_pos = lax.dynamic_slice_in_dim(key_pos, start, block, 0)
        block_ok = lax.dynamic_slice_in_dim(key_ok, start, block, 0)
        scores = (
            jnp.einsum("tgrd,gdk->tgrk", queries, block_keys, preferred_element_type=jnp.float32)
            * scale
        )
        allowed = (
            block_ok[None, :]
            & (block_pos[None, :] <= query_pos[:, None])
            & (query_pos[:, None] - block_pos[None, :] < WIN)
        )
        allowed = allowed[:, None, None, :]
        top_new = jnp.maximum(top_old, jnp.max(jnp.where(allowed, scores, LOWEST), axis=-1))
        weights = jnp.where(allowed, jnp.exp(scores - top_new[..., None]), 0.0)
        rescale = jnp.exp(top_old - top_new)
        sum_new = sum_old * rescale + jnp.sum(weights, axis=-1)
        mixed = jnp.einsum(
            "tgrk,gdk->tgrd",
            weights.astype(jnp.bfloat16),
            block_values,
            preferred_element_type=jnp.float32,
        )
        return (accum * rescale[..., None] + mixed, top_new, sum_new)

    return lax.fori_loop(0, key_count // block, step, state)


def shards(
    tokens_in,
    norm_gain,
    query_weight,
    key_weight,
    value_weight,
    out_weight,
    cache_keys,
    cache_values,
    cached_len,
    append_slot,
    shard_owner,
):
    whole = lax.all_gather(tokens_in, "narrow", axis=1, tiled=True)
    normed = rms_normed(whole, norm_gain)
    tok_rows = whole.shape[0]
    query_width = query_weight.shape[1]
    kv_width = key_weight.shape[1]
    local_heads = query_width // HEAD_DIM
    local_groups = kv_width // HEAD_DIM
    repeats = local_heads // local_groups
    columns = normed
    query_sum = jnp.dot(
        columns,
        lax.all_gather(query_weight, "wide", axis=0, tiled=True),
        preferred_element_type=jnp.float32,
    )
    key_sum = jnp.dot(
        columns,
        lax.all_gather(key_weight, "wide", axis=0, tiled=True),
        preferred_element_type=jnp.float32,
    )
    value_sum = jnp.dot(
        columns,
        lax.all_gather(value_weight, "wide", axis=0, tiled=True),
        preferred_element_type=jnp.float32,
    )
    position = lax.axis_index("wide")
    request = position // GROUP
    place = position % GROUP
    length = cached_len[request]
    offset = append_slot[request]
    owner = shard_owner[request]
    query_pos = length + place * tok_rows + jnp.arange(tok_rows, dtype=jnp.int32)
    queries = rotate(query_sum.reshape(tok_rows, local_heads, HEAD_DIM), query_pos).astype(
        jnp.bfloat16
    )
    queries = queries.reshape(tok_rows, local_groups, repeats, HEAD_DIM)
    new_keys = (
        rotate(key_sum.reshape(tok_rows, local_groups, HEAD_DIM), query_pos)
        .astype(jnp.bfloat16)
        .reshape(tok_rows, kv_width)
    )
    new_values = value_sum.astype(jnp.bfloat16)
    shard_rows = cache_keys.shape[1]
    within = jnp.arange(shard_rows, dtype=jnp.int32)
    cycle_mine = (place - owner) % GROUP * shard_rows + within
    old_keys, old_values = (cache_keys, cache_values)
    for bit in range(GROUP_BITS):
        upper = place // 2**bit % 2 == 1
        other_keys, other_values, other_old_keys, other_old_values = from_partner(
            (new_keys, new_values, old_keys, old_values), "wide", bit
        )
        new_keys = ordered(new_keys, other_keys, upper, 0)
        new_values = ordered(new_values, other_values, upper, 0)
        old_keys = ordered(old_keys, other_old_keys, upper, 1)
        old_values = ordered(old_values, other_old_values, upper, 1)
    slot_index = jnp.arange(old_keys.shape[1], dtype=jnp.int32)
    cycle = (slot_index // shard_rows - owner) % GROUP * shard_rows + slot_index % shard_rows
    cached_pos = (cycle - offset + length) % WIN
    state = fold_keys(
        empty_state(tok_rows, local_groups, repeats),
        queries,
        query_pos,
        old_keys,
        old_values,
        cached_pos,
        cached_pos < length,
        512,
    )
    key_cols = new_keys.T
    value_cols = new_values.T
    new_count = key_cols.shape[1]
    new_pos = length + jnp.arange(new_count, dtype=jnp.int32)
    state = fold_keys(
        state,
        queries,
        query_pos,
        key_cols,
        value_cols,
        new_pos,
        jnp.ones((new_count,), dtype=bool),
        512,
    )
    accum, top_score, total = state
    attended = (accum / total[..., None]).astype(jnp.bfloat16).reshape(tok_rows, query_width)
    all_heads = lax.all_gather(attended, "narrow", axis=1, tiled=True)
    columns = all_heads
    update = jnp.dot(
        columns,
        lax.all_gather(out_weight, "wide", axis=0, tiled=True),
        preferred_element_type=jnp.float32,
    ).astype(jnp.bfloat16)
    new_index = (cycle_mine - offset) % WIN
    written = new_index < new_count
    take_rows = jnp.minimum(new_index, new_count - 1)
    put_keys = jnp.where(written[None, :], jnp.take(key_cols, take_rows, axis=1), cache_keys)
    put_values = jnp.where(written[None, :], jnp.take(value_cols, take_rows, axis=1), cache_values)
    return (update, put_keys, put_values)


def solution(mesh):
    in_specs = (
        P("wide", "narrow"),
        P(),
        P("wide", "narrow"),
        P("wide", "narrow"),
        P("wide", "narrow"),
        P("wide", "narrow"),
        P("narrow", "wide"),
        P("narrow", "wide"),
        P(),
        P(),
        P(),
    )
    out_specs = (P("wide", "narrow"), P("narrow", "wide"), P("narrow", "wide"))
    return jax.shard_map(shards, mesh=mesh, in_specs=in_specs, out_specs=out_specs, check_vma=False)
```

profile of v0, /device:TPU:1, one launch (start us, length us, event | category | flops | bytes accessed | tf_op | source)
XLA Modules:
  0.0 399.1 jit_solution(11105308332598685223)
XLA Ops:
  8.0 109.3 %all-gather.2 = bf16[128,20,160]{2,1,0:T(8,128)(2,1)S(1)} all-gather(bf16[1,20,160]{2,1,0:T(8,128)(2,1)} %bitcast.135), channel_id=1, replica_groups=mesh['wide'=128,'narrow'=4] {'wide'}, dimensions={0}, use_global_device_ids=true | all-gather | bytes 825600 | tf_op jit(solution)/shard_map/all_gather | solution.py:133
  117.9 12.4 %all_gather.18 = bf16[128,2560]{1,0:T(8,128)(2,1)S(1)} all-gather(bf16[128,640]{1,0:T(8,128)(2,1)} %param.15), channel_id=1, replica_groups=mesh['wide'=128,'narrow'=4] {'narrow'}, dimensions={1}, use_global_device_ids=true | all-gather | bytes 819200 | tf_op jit(solution)/shard_map/all_gather | solution.py:112
  130.6 1.2 convolution_convert_fusion.1
  131.8 4.1 %collective-permute-start.6 = (bf16[128,160]{0,1:T(8,128)(2,1)}, bf16[128,160]{0,1:T(8,128)(2,1)}, u32[]{:S(2)}, u32[]{:S(2)}) collective-permute-start(bf16[128,160]{0,1:T(8,128)(2,1)} %convolution_convert_fusion.1), channel_id=1, source_target_pairs={{0,4},{4,0},{8,12},{12,8},{16,20},{20,16},{24,28},{28,24},{32,36},... | collective-permute-start | bytes 122888 | tf_op jit(solution)/shard_map/ppermute | solution.py:23
  135.9 100.1 %all-gather.1 = bf16[128,20,160]{2,1,0:T(8,128)(2,1)S(1)} all-gather(bf16[1,20,160]{2,1,0:T(8,128)(2,1)} %bitcast.136), channel_id=1, replica_groups=mesh['wide'=128,'narrow'=4] {'wide'}, dimensions={0}, use_global_device_ids=true | all-gather | bytes 825600 | tf_op jit(solution)/shard_map/all_gather | solution.py:128
  236.7 1.3 dynamic_slice.45
  239.4 2.1 collective-permute-start.4
  241.5 2.3 collective-permute-start.2
  243.8 2.3 collective-permute-start
  248.0 2.5 broadcast_compare_fusion
  250.5 2.5 add_select_fusion
  253.7 1.2 fusion.54
  255.7 1.2 compare_and_fusion
  259.2 1.9 collective-permute-start.7
  261.2 3.4 collective-permute-start.5
  265.8 1.2 collective-permute-done.5
  267.8 1.4 broadcast_select_fusion.5
  270.1 2.8 collective-permute-start.1
  274.7 5.3 %gather_fusion.1 = bf16[1024,160]{1,0:T(8,128)(2,1)} fusion(bf16[160,512]{0,1:T(8,128)(2,1)S(1)} %copy.40, s32[1024]{0:T(1024)} %fusion.54), kind=kCustom, calls=%fused_computation.1.clone | custom fusion | bytes 659456 | tf_op jit(solution)/shard_map/jit(_take)/gather | solution.py:206
  280.0 5.3 %gather_fusion = bf16[1024,160]{1,0:T(8,128)(2,1)} fusion(bf16[160,512]{0,1:T(8,128)(2,1)S(1)} %copy.38, s32[1024]{0:T(1024)} %fusion.54), kind=kCustom, calls=%fused_computation.clone | custom fusion | bytes 659456 | tf_op jit(solution)/shard_map/jit(_take)/gather | solution.py:205
  285.3 2.5 bitcast_select_fusion.2
  287.8 1.9 copy.42
  290.7 2.4 collective-permute-start.3
  293.2 1.4 broadcast_select_fusion.3
  295.8 11.1 %collective-permute-done.3 = bf16[160,2048]{1,0:T(8,128)(2,1)S(1)} collective-permute-done((bf16[160,2048]{1,0:T(8,128)(2,1)S(1)}, bf16[160,2048]{1,0:T(8,128)(2,1)S(1)}, u32[]{:S(2)}, u32[]{:S(2)}) %collective-permute-start.3) | collective-permute-done | bytes 655392 | tf_op jit(solution)/shard_map/ppermute | solution.py:23
  308.4 6.1 %reshape.265 = bf16[2560,640]{1,0:T(8,128)(2,1)} reshape(bf16[128,20,640]{2,1,0:T(8,128)(2,1)} %all-gather.7.cloned.1.call-done) | data formatting | bytes 6553600
  314.5 3.4 fusion.64
  318.1 41.1 %while.5 = (s32[]{:T(128)}, f32[128,2,4,80]{0,3,2,1:T(8,128)S(1)}, f32[128,2,4]{0,2,1:T(4,128)S(1)}, f32[128,2,4]{0,2,1:T(4,128)S(1)}, pred[4096]{0:T(1024)(128)...) while((s32[]{:T(128)}, f32[128,2,4,80]{0,3,2,1:T(8,128)S(1)}, ...), condition=%wide.region_4.5_spmd.clone, body=%wide.region_1.4_spmd.clone.sunk | while | flops 174118016 | bytes 7774939 | solution.py:96
  319.8 1.4 fusion.86
  321.7 1.5 fusion.89
  324.9 1.4 fusion.86
  326.8 1.5 fusion.89
  329.9 1.4 fusion.86
  331.9 1.5 fusion.89
  335.0 1.4 fusion.86
  337.0 1.5 fusion.89
  340.2 1.4 fusion.86
  342.1 1.5 fusion.89
  345.4 1.4 fusion.86
  347.3 1.5 fusion.89
  350.6 1.4 fusion.86
  352.5 1.5 fusion.89
  355.7 1.4 fusion.86
  357.6 1.5 fusion.89
  360.7 11.0 %all_gather.22 = bf16[128,2560]{0,1:T(8,128)(2,1)S(1)} all-gather(bf16[128,640]{0,1:T(8,128)(2,1)S(1)} %bitcast.129), channel_id=1, replica_groups=mesh['wide'=128,'narrow'=4] {'narrow'}, dimensions={1}, use_global_device_ids=true | all-gather | bytes 819200 | tf_op jit(solution)/shard_map/all_gather | solution.py:195
  371.7 11.2 %all-gather.9.cloned.1.call-done = bf16[128,20,640]{2,1,0:T(8,128)(2,1)} async-done(((bf16[1,20,640]{2,1,0:T(8,128)(2,1)}), bf16[128,20,640]{2,1,0:T(8,128)(2,1)}) %all-gather.9.cloned.1.call-update) | async-done | bytes 3276816 | tf_op jit(solution)/shard_map/all_gather | solution.py:199
  382.9 6.1 %reshape.271 = bf16[2560,640]{1,0:T(8,128)(2,1)} reshape(bf16[128,20,640]{2,1,0:T(8,128)(2,1)} %all-gather.9.cloned.1.call-done) | data formatting | bytes 6553600
  389.0 3.3 convolution_convert_fusion
  (150 shorter events, 35.2 us)
Async XLA Ops:
  7.2 301.2 %all-gather.7.cloned.1.call-start = ((), (), s32[]{:S(2)}) async-start(), calls=%async_computation | async-start | bytes 3962880 | tf_op jit(solution)/shard_map/all_gather | solution.py:123
  7.9 375.0 %all-gather.9.cloned.1.call-start = ((), (), s32[]{:S(2)}) async-start(), calls=%async_computation.1 | async-start | bytes 3962880 | tf_op jit(solution)/shard_map/all_gather | solution.py:199
  7.9 109.9 %copy-start.10 = (bf16[2560]{0:T(1024)(128)(2,1)S(1)}, bf16[2560]{0:T(1024)(128)(2,1)}, u32[]{:S(2)}) copy-start(bf16[2560]{0:T(1024)(128)(2,1)} %param.16) | copy-start | bytes 15364
  130.5 108.2 %copy-start.11 = (f32[128]{0:T(128)}, f32[128]{0:T(128)S(1)}, u32[]{:S(2)}) copy-start(f32[128]{0:T(128)S(1)} %add_rsqrt_fusion) | copy-start | bytes 1540
  131.8 126.6 %collective-permute-start.6 = (bf16[128,160]{0,1:T(8,128)(2,1)}, bf16[128,160]{0,1:T(8,128)(2,1)}, u32[]{:S(2)}, u32[]{:S(2)}) collective-permute-start(bf16[128,160]{0,1:T(8,128)(2,1)} %convolution_convert_fusion.1), channel_id=1, source_target_pairs={{0,4},{4,0},{8,12},{12,8},{16,20},{20,16},{24,28},{28,24},{32,36},... | collective-permute-start | bytes 122888 | tf_op jit(solution)/shard_map/ppermute | solution.py:23
  236.6 4.9 %copy-start = (bf16[160,1024]{1,0:T(8,128)(2,1)S(1)}, bf16[160,1024]{1,0:T(8,128)(2,1)}, u32[]{:S(2)}) copy-start(bf16[160,1024]{1,0:T(8,128)(2,1)} %param.22) | copy-start | bytes 983044
  236.6 10.1 %copy-start.13 = (s32[32]{0:T(128)S(1)}, s32[32]{0:T(128)}, u32[]{:S(2)}) copy-start(s32[32]{0:T(128)} %param.24) | copy-start | bytes 388
  236.6 10.8 %copy-start.14 = (s32[32]{0:T(128)S(1)}, s32[32]{0:T(128)}, u32[]{:S(2)}) copy-start(s32[32]{0:T(128)} %param.25) | copy-start | bytes 388
  238.8 19.6 %copy-start.4 = (f32[128,40]{0,1:T(8,128)}, f32[128,40]{0,1:T(8,128)S(1)}, u32[]{:S(2)}) copy-start(f32[128,40]{0,1:T(8,128)S(1)} %get-tuple-element.305) | copy-start | bytes 61444
  238.8 19.6 %copy-start.6 = (f32[128,40]{0,1:T(8,128)}, f32[128,40]{0,1:T(8,128)S(1)}, u32[]{:S(2)}) copy-start(f32[128,40]{0,1:T(8,128)S(1)} %get-tuple-element.306) | copy-start | bytes 61444
  239.4 18.9 %collective-permute-start.4 = (bf16[128,160]{0,1:T(8,128)(2,1)S(1)}, bf16[128,160]{0,1:T(8,128)(2,1)S(1)}, u32[]{:S(2)}, u32[]{:S(2)}) collective-permute-start(bf16[128,160]{0,1:T(8,128)(2,1)S(1)} %bitcast.127), channel_id=1, source_target_pairs={{0,4},{4,0},{8,12},{12,8},{16,20},{20,16},{24,28},{28,24},{32,36},... | collective-permute-start | bytes 122888 | tf_op jit(solution)/shard_map/ppermute | solution.py:23
  241.5 25.5 %collective-permute-start.2 = (bf16[160,1024]{1,0:T(8,128)(2,1)S(1)}, bf16[160,1024]{1,0:T(8,128)(2,1)S(1)}, u32[]{:S(2)}, u32[]{:S(2)}) collective-permute-start(bf16[160,1024]{1,0:T(8,128)(2,1)S(1)} %copy-done), channel_id=1, source_target_pairs={{0,4},{4,0},{8,12},{12,8},{16,20},{20,16},{24,28},{28,24},{32,36},... | collective-permute-start | bytes 983048 | tf_op jit(solution)/shard_map/ppermute | solution.py:23
  243.8 24.0 %collective-permute-start = (bf16[160,1024]{1,0:T(8,128)(2,1)}, bf16[160,1024]{1,0:T(8,128)(2,1)}, u32[]{:S(2)}, u32[]{:S(2)}) collective-permute-start(bf16[160,1024]{1,0:T(8,128)(2,1)} %param.21), channel_id=1, source_target_pairs={{0,4},{4,0},{8,12},{12,8},{16,20},{20,16},{24,28},{28,24},{32,36},... | collective-permute-start | bytes 983048 | tf_op jit(solution)/shard_map/ppermute | solution.py:23
  259.2 5.7 %collective-permute-start.7 = (bf16[256,160]{0,1:T(8,128)(2,1)S(1)}, bf16[256,160]{0,1:T(8,128)(2,1)S(1)}, u32[]{:S(2)}, u32[]{:S(2)}) collective-permute-start(bf16[256,160]{0,1:T(8,128)(2,1)S(1)} %pad_maximum_fusion.8), channel_id=1, source_target_pairs={{0,8},{8,0},{4,12},{12,4},{16,24},{24,16},{20,28},{28,20},{32,40},... | collective-permute-start | bytes 245768 | tf_op jit(solution)/shard_map/ppermute | solution.py:23
  261.2 5.8 %collective-permute-start.5 = (bf16[256,160]{0,1:T(8,128)(2,1)S(1)}, bf16[256,160]{0,1:T(8,128)(2,1)S(1)}, u32[]{:S(2)}, u32[]{:S(2)}) collective-permute-start(bf16[256,160]{0,1:T(8,128)(2,1)S(1)} %pad_maximum_fusion.7), channel_id=1, source_target_pairs={{0,8},{8,0},{4,12},{12,4},{16,24},{24,16},{20,28},{28,20},{32,40},... | collective-permute-start | bytes 245768 | tf_op jit(solution)/shard_map/ppermute | solution.py:23
  267.0 0.7 copy-start.3
  270.1 23.1 %collective-permute-start.1 = (bf16[160,2048]{1,0:T(8,128)(2,1)}, bf16[160,2048]{1,0:T(8,128)(2,1)}, u32[]{:S(2)}, u32[]{:S(2)}) collective-permute-start(bf16[160,2048]{1,0:T(8,128)(2,1)} %pad_maximum_fusion.2), channel_id=1, source_target_pairs={{0,8},{8,0},{4,12},{12,4},{16,24},{24,16},{20,28},{28,20},{32,40},... | collective-permute-start | bytes 1966088 | tf_op jit(solution)/shard_map/ppermute | solution.py:23
  290.7 16.2 %collective-permute-start.3 = (bf16[160,2048]{1,0:T(8,128)(2,1)S(1)}, bf16[160,2048]{1,0:T(8,128)(2,1)S(1)}, u32[]{:S(2)}, u32[]{:S(2)}) collective-permute-start(bf16[160,2048]{1,0:T(8,128)(2,1)S(1)} %pad_maximum_fusion.3), channel_id=1, source_target_pairs={{0,8},{8,0},{4,12},{12,4},{16,24},{24,16},{20,28},{28,20},{32,40},... | collective-permute-start | bytes 1966088 | tf_op jit(solution)/shard_map/ppermute | solution.py:23
  308.4 6.1 %copy-start.12 = (f32[128]{0:T(128)S(1)}, f32[128]{0:T(128)}, u32[]{:S(2)}) copy-start(f32[128]{0:T(128)} %copy-done.11) | copy-start | bytes 1540
  314.5 3.4 copy-start.5
  314.5 3.4 copy-start.7
  314.5 3.5 copy-start.9
  314.5 3.5 copy-start.15
  318.0 41.1 %copy-start.1 = (bf16[512,160]{0,1:T(8,128)(2,1)S(1)}, bf16[512,160]{0,1:T(8,128)(2,1)}, u32[]{:S(2)}) copy-start(bf16[512,160]{0,1:T(8,128)(2,1)} %get-tuple-element.292) | copy-start | bytes 491524
  318.0 41.1 %copy-start.2 = (pred[128,512]{0,1:T(8,128)(4,1)S(1)}, pred[128,512]{0,1:T(8,128)(4,1)}, u32[]{:S(2)}) copy-start(pred[128,512]{0,1:T(8,128)(4,1)} %fusion.38) | copy-start | bytes 196612
  359.2 1.0 copy-start.8
Sparse Core Ops, SparseCore 0:
  11.0 147.4 all-gather.6
  246.2 136.6 all-gather.8
where the time goes:
time: 401 us; the launch traced here: 399 us
  blocking collectives  233 us (58%)
  local copies, waits for them, and re-layouts  44.6 us (11%)
  matrix products  32.8 us (8%)
  other arithmetic  26.6 us (7%)
  waiting for transfers between devices  24.6 us (6%)
  starting transfers between devices  21.3 us (5%)
  between operations  15.9 us (4%)
    all_gather x1, blocking collectives, shards(): lax.all_gather(value_weight, 'wide', axis=0, tiled=True)  109 us
    all_gather x1, blocking collectives, shards(): lax.all_gather(key_weight, 'wide', axis=0, tiled=True)  100 us
    ppermute x8, starting transfers between devices, from_partner(): return lax.ppermute(block, axis, route)  21.2 us
    unnamed x40, local copies, waits for them, and re-layouts  18.5 us
    ppermute x8, waiting for transfers between devices, from_partner(): return lax.ppermute(block, axis, route)  12.7 us
    all_gather x1, blocking collectives, shards(): whole = lax.all_gather(tokens_in, 'narrow', axis=1, tiled=True)  12.4 us
    dot_general x9, matrix products, step(): jnp.einsum('tgrk,gdk->tgrd', weights.astype(jnp.bfloat16), block_values,...  12.2 us
    dot_general x9, matrix products, step(): jnp.einsum('tgrd,gdk->tgrk', queries, block_keys, preferred_element_type=...  12 us
  transfers between devices with their start and end apart: 10, of which 4 were waited for; matrix products, arithmetic and copies ran while one was open for 23% of the time, Pallas kernels for 0%

commit v1 on v0

--- a/solution.py
+++ b/solution.py
@@ -1,8 +1,10 @@
+import functools
 import math
 import jax
 import jax.numpy as jnp
 from jax import lax
 from jax.sharding import PartitionSpec as P
+from jax.lax import axis_index, axis_size, ppermute
 
 HEAD_DIM = 80
 WIN = 4096
@@ -11,6 +13,22 @@
 EPSILON = 1e-05
 ROPE_BASE = 10000.0
 LOWEST = -1e30
+
+
+def squares_put(local_block, device_axis):
+    parts_n = axis_size(device_axis)
+    built = [None] * parts_n
+    built[parts_n - 1] = local_block
+    panels = [(m, (m + 1) % parts_n) for m in range(parts_n)]
+    for at in range(parts_n - 2, -1, -1):
+        built[at] = ppermute(built[at + 1], device_axis, perm=panels)
+    parts_out = jnp.concatenate(built, 1)
+    local_next = axis_index(device_axis)
+    even = (local_next + 1) * local_block.shape[1]
+    return jnp.roll(parts_out, even, 1)
+
+
+reach_heaps = functools.partial(squares_put, device_axis="narrow")
 
 
 def from_partner(block, axis, bit):
@@ -109,7 +127,7 @@
     append_slot,
     shard_owner,
 ):
-    whole = lax.all_gather(tokens_in, "narrow", axis=1, tiled=True)
+    whole = reach_heaps(tokens_in)
     normed = rms_normed(whole, norm_gain)
     tok_rows = whole.shape[0]
     query_width = query_weight.shape[1]

time: 401 us -> 401 us (level)
  blocking collectives: 233 us -> 217 us
  starting transfers between devices: 21.3 us -> 33.3 us
  local copies, waits for them, and re-layouts: 44.6 us -> 55.9 us
  waiting for transfers between devices: 24.6 us -> 16.4 us
    all_gather x1 -> x0, blocking collectives: 12.4 us -> none  [shards(): whole = lax.all_gather(tokens_in, 'narrow', axis=1, tiled=True)]
    all_gather x1, waiting for transfers between devices: 11.2 us -> 0.01 us  [shards(): lax.all_gather(out_weight, 'wide', axis=0, tiled=True)]
    ppermute x0 -> x3, starting transfers between devices: none -> 10.2 us  [squares_put(): built[at] = ppermute(built[at + 1], device_axis, perm=panels)]
    while x8 -> x40, local copies, waits for them, and re-layouts: 0.02 us -> 9.69 us
    all_gather x1, blocking collectives: 109 us -> 105 us  [shards(): lax.all_gather(value_weight, 'wide', axis=0, tiled=True)]
    unnamed x40 -> x61, local copies, waits for them, and re-layouts: 18.5 us -> 21.8 us
  transfers between devices with their start and end apart: 10 -> 13, of which waited for: 4 -> 3; matrix products, arithmetic and copies ran while one was open for 23% -> 24% of each run, Pallas kernels for 0% -> 0%
where the time goes in v1:
time: 401 us; the launch traced here: 398 us
  blocking collectives  217 us (54%)
  local copies, waits for them, and re-layouts  55.9 us (14%)
  starting transfers between devices  33.3 us (8%)
  matrix products  31 us (8%)
  other arithmetic  27.8 us (7%)
  waiting for transfers between devices  16.4 us (4%)
  between operations  16 us (4%)
    all_gather x1, blocking collectives, shards(): lax.all_gather(value_weight, 'wide', axis=0, tiled=True)  105 us
    all_gather x1, blocking collectives, shards(): lax.all_gather(key_weight, 'wide', axis=0, tiled=True)  100 us
    ppermute x8, starting transfers between devices, from_partner(): return lax.ppermute(block, axis, route)  23.1 us
    unnamed x61, local copies, waits for them, and re-layouts  21.8 us
    ppermute x8, waiting for transfers between devices, from_partner(): return lax.ppermute(block, axis, route)  14.3 us
    dot_general x9, matrix products, step(): jnp.einsum('tgrk,gdk->tgrd', weights.astype(jnp.bfloat16), block_values,...  12.2 us
    dot_general x9, matrix products, step(): jnp.einsum('tgrd,gdk->tgrk', queries, block_keys, preferred_element_type=...  12 us
    all_gather x1, blocking collectives, shards(): all_heads = lax.all_gather(attended, 'narrow', axis=1, tiled=True)  11.9 us
  transfers between devices with their start and end apart: 13, of which 3 were waited for; matrix products, arithmetic and copies ran while one was open for 24% of the time, Pallas kernels for 0%

profile of v1, /device:TPU:1, one launch (start us, length us, event | category | flops | bytes accessed | tf_op | source)
XLA Modules:
  0.0 397.8 jit_solution(2868213210408274112)
XLA Ops:
  8.0 4.0 %collective-permute-start.2 = (bf16[128,640]{1,0:T(8,128)(2,1)}, bf16[128,640]{1,0:T(8,128)(2,1)}, u32[]{:S(2)}, u32[]{:S(2)}) collective-permute-start(bf16[128,640]{1,0:T(8,128)(2,1)} %param.15), channel_id=1, source_target_pairs={{0,1},{1,2},{2,3},{3,0},{4,5},{5,6},{6,7},{7,4},{8,9},{9,10},{10,1... | collective-permute-start | bytes 491528 | tf_op jit(solution)/shard_map/ppermute | solution.py:24
  12.0 6.7 %collective-permute-start.5 = (bf16[160,1024]{1,0:T(8,128)(2,1)}, bf16[160,1024]{1,0:T(8,128)(2,1)}, u32[]{:S(2)}, u32[]{:S(2)}) collective-permute-start(bf16[160,1024]{1,0:T(8,128)(2,1)} %param.22), channel_id=1, source_target_pairs={{0,4},{4,0},{8,12},{12,8},{16,20},{20,16},{24,28},{28,24},{32,36},... | collective-permute-start | bytes 983048 | tf_op jit(solution)/shard_map/ppermute | solution.py:41
  18.7 1.9 collective-permute-start
  23.3 104.8 %all-gather.2 = bf16[128,20,160]{2,1,0:T(8,128)(2,1)S(1)} all-gather(bf16[1,20,160]{2,1,0:T(8,128)(2,1)} %bitcast.135), channel_id=1, replica_groups=mesh['wide'=128,'narrow'=4] {'wide'}, dimensions={0}, use_global_device_ids=true | all-gather | bytes 825600 | tf_op jit(solution)/shard_map/all_gather | solution.py:151
  128.1 100.1 %all-gather.1 = bf16[128,20,160]{2,1,0:T(8,128)(2,1)S(1)} all-gather(bf16[1,20,160]{2,1,0:T(8,128)(2,1)S(1)} %bitcast.136), channel_id=1, replica_groups=mesh['wide'=128,'narrow'=4] {'wide'}, dimensions={0}, use_global_device_ids=true | all-gather | bytes 825600 | tf_op jit(solution)/shard_map/all_gather | solution.py:146
  230.9 2.5 broadcast_compare_fusion
  234.1 1.3 fusion.54
  235.4 3.2 collective-permute-start.3
  240.9 2.0 copy.39
  242.9 1.5 reshape.269
  245.0 2.5 add_select_fusion
  247.5 2.9 collective-permute-start.4
  252.6 2.1 collective-permute-start.1
  254.7 1.5 collective-permute-done.4
  261.5 3.3 collective-permute-start.9
  265.6 1.9 collective-permute-start.7
  268.5 1.9 collective-permute-start.6
  270.5 3.4 collective-permute-start.10
  273.9 1.9 collective-permute-start.8
  275.8 13.5 %collective-permute-done.10 = bf16[256,160]{0,1:T(8,128)(2,1)S(1)} collective-permute-done((bf16[256,160]{0,1:T(8,128)(2,1)S(1)}, bf16[256,160]{0,1:T(8,128)(2,1)S(1)}, u32[]{:S(2)}, u32[]{:S(2)}) %collective-permute-start.10) | collective-permute-done | bytes 81952 | tf_op jit(solution)/shard_map/ppermute | solution.py:41
  291.2 4.9 %gather_fusion.1 = bf16[1024,160]{1,0:T(8,128)(2,1)} fusion(bf16[160,512]{0,1:T(8,128)(2,1)S(1)} %copy.40, s32[1024]{0:T(1024)S(1)} %copy-done.13), kind=kCustom, calls=%fused_computation.1.clone | custom fusion | bytes 659456 | tf_op jit(solution)/shard_map/jit(_take)/gather | solution.py:224
  296.1 4.9 %gather_fusion = bf16[1024,160]{1,0:T(8,128)(2,1)} fusion(bf16[160,512]{0,1:T(8,128)(2,1)S(1)} %copy.38, s32[1024]{0:T(1024)S(1)} %copy-done.13), kind=kCustom, calls=%fused_computation.clone | custom fusion | bytes 659456 | tf_op jit(solution)/shard_map/jit(_take)/gather | solution.py:223
  301.1 2.6 bitcast_select_fusion.2
  303.6 1.9 copy.42
  306.5 1.4 broadcast_select_fusion.3
  309.1 1.4 broadcast_select_fusion.1
  311.6 4.6 %reshape.265 = bf16[2560,640]{1,0:T(8,128)(2,1)S(1)} reshape(bf16[128,20,640]{2,1,0:T(8,128)(2,1)} %all-gather.7.cloned.1.call-done) | data formatting | bytes 6553600
  316.3 2.8 fusion.64
  319.2 50.6 %while.5 = (s32[]{:T(128)}, f32[128,2,4,80]{0,3,2,1:T(8,128)}, f32[128,2,4]{0,2,1:T(4,128)S(1)}, f32[128,2,4]{0,2,1:T(4,128)S(1)}, pred[4096]{0:T(1024)(128)(4,1...) while((s32[]{:T(128)}, f32[128,2,4,80]{0,3,2,1:T(8,128)}, ...), condition=%wide.region_4.5_spmd.clone, body=%wide.region_1.4_spmd.clone.sunk | while | flops 174118016 | bytes 10396435 | solution.py:114
  320.9 1.4 fusion.86
  323.3 1.5 fusion.89
  327.2 1.4 fusion.86
  329.6 1.5 fusion.89
  333.5 1.4 fusion.86
  336.0 1.5 fusion.89
  339.9 1.4 fusion.86
  342.3 1.5 fusion.89
  346.2 1.4 fusion.86
  348.6 1.5 fusion.89
  352.5 1.4 fusion.86
  355.0 1.5 fusion.89
  358.8 1.4 fusion.86
  361.3 1.5 fusion.89
  365.1 1.4 fusion.86
  367.6 1.5 fusion.89
  371.9 11.9 %all_gather.18 = bf16[128,2560]{0,1:T(8,128)(2,1)} all-gather(bf16[128,640]{0,1:T(8,128)(2,1)S(1)} %bitcast.129), channel_id=1, replica_groups=mesh['wide'=128,'narrow'=4] {'narrow'}, dimensions={1}, use_global_device_ids=true | all-gather | bytes 819200 | tf_op jit(solution)/shard_map/all_gather | solution.py:213
  383.8 4.6 %reshape.271 = bf16[2560,640]{1,0:T(8,128)(2,1)S(1)} reshape(bf16[128,20,640]{2,1,0:T(8,128)(2,1)} %all-gather.9.cloned.1.call-done) | data formatting | bytes 6553600
  388.5 2.5 convolution_convert_fusion
  (209 shorter events, 51.6 us)
Async XLA Ops:
  7.2 120.9 %copy-start.14 = (bf16[20,160]{1,0:T(8,128)(2,1)S(1)}, bf16[20,160]{1,0:T(8,128)(2,1)}, u32[]{:S(2)}) copy-start(bf16[20,160]{1,0:T(8,128)(2,1)} %param.18) | copy-start | bytes 19204
  7.2 304.4 %all-gather.7.cloned.1.call-start = ((), (), s32[]{:S(2)}) async-start(), calls=%async_computation | async-start | bytes 3962880 | tf_op jit(solution)/shard_map/all_gather | solution.py:141
  7.9 375.9 %all-gather.9.cloned.1.call-start = ((), (), s32[]{:S(2)}) async-start(), calls=%async_computation.1 | async-start | bytes 3962880 | tf_op jit(solution)/shard_map/all_gather | solution.py:217
  8.0 227.4 %collective-permute-start.2 = (bf16[128,640]{1,0:T(8,128)(2,1)}, bf16[128,640]{1,0:T(8,128)(2,1)}, u32[]{:S(2)}, u32[]{:S(2)}) collective-permute-start(bf16[128,640]{1,0:T(8,128)(2,1)} %param.15), channel_id=1, source_target_pairs={{0,1},{1,2},{2,3},{3,0},{4,5},{5,6},{6,7},{7,4},{8,9},{9,10},{10,1... | collective-permute-start | bytes 491528 | tf_op jit(solution)/shard_map/ppermute | solution.py:24
  12.0 238.4 %collective-permute-start.5 = (bf16[160,1024]{1,0:T(8,128)(2,1)}, bf16[160,1024]{1,0:T(8,128)(2,1)}, u32[]{:S(2)}, u32[]{:S(2)}) collective-permute-start(bf16[160,1024]{1,0:T(8,128)(2,1)} %param.22), channel_id=1, source_target_pairs={{0,4},{4,0},{8,12},{12,8},{16,20},{20,16},{24,28},{28,24},{32,36},... | collective-permute-start | bytes 983048 | tf_op jit(solution)/shard_map/ppermute | solution.py:41
  18.7 231.8 %collective-permute-start = (bf16[160,1024]{1,0:T(8,128)(2,1)}, bf16[160,1024]{1,0:T(8,128)(2,1)}, u32[]{:S(2)}, u32[]{:S(2)}) collective-permute-start(bf16[160,1024]{1,0:T(8,128)(2,1)} %param.21), channel_id=1, source_target_pairs={{0,4},{4,0},{8,12},{12,8},{16,20},{20,16},{24,28},{28,24},{32,36},... | collective-permute-start | bytes 983048 | tf_op jit(solution)/shard_map/ppermute | solution.py:41
  23.3 204.8 %copy-start.20 = (s32[32]{0:T(128)S(1)}, s32[32]{0:T(128)}, u32[]{:S(2)}) copy-start(s32[32]{0:T(128)} %param.24) | copy-start | bytes 388
  23.3 205.5 %copy-start.21 = (s32[32]{0:T(128)S(1)}, s32[32]{0:T(128)}, u32[]{:S(2)}) copy-start(s32[32]{0:T(128)} %param.25) | copy-start | bytes 388
  23.3 216.6 %copy-start.4 = (bf16[160,1024]{1,0:T(8,128)(2,1)S(1)}, bf16[160,1024]{1,0:T(8,128)(2,1)}, u32[]{:S(2)}) copy-start(bf16[160,1024]{1,0:T(8,128)(2,1)} %param.22) | copy-start | bytes 983044
  235.4 12.2 %collective-permute-start.3 = (bf16[128,640]{1,0:T(8,128)(2,1)}, bf16[128,640]{1,0:T(8,128)(2,1)}, u32[]{:S(2)}, u32[]{:S(2)}) collective-permute-start(bf16[128,640]{1,0:T(8,128)(2,1)} %collective-permute-done.2), channel_id=1, source_target_pairs={{0,1},{1,2},{2,3},{3,0},{4,5},{5,6},{6,7},{7,4},{8,9},{9,10},{10,1... | collective-permute-start | bytes 491528 | tf_op jit(solution)/shard_map/ppermute | solution.py:24
  242.9 1.5 copy-start.15
  247.5 8.6 %collective-permute-start.4 = (bf16[128,640]{1,0:T(8,128)(2,1)}, bf16[128,640]{1,0:T(8,128)(2,1)S(1)}, u32[]{:S(2)}, u32[]{:S(2)}) collective-permute-start(bf16[128,640]{1,0:T(8,128)(2,1)} %collective-permute-done.3), channel_id=1, source_target_pairs={{0,1},{1,2},{2,3},{3,0},{4,5},{5,6},{6,7},{7,4},{8,9},{9,10},{10,1... | collective-permute-start | bytes 491528 | tf_op jit(solution)/shard_map/ppermute | solution.py:24
  251.7 6.5 %copy-start.5 = (bf16[128,640]{1,0:T(8,128)(2,1)S(1)}, bf16[128,640]{1,0:T(8,128)(2,1)}, u32[]{:S(2)}) copy-start(bf16[128,640]{1,0:T(8,128)(2,1)} %param.15) | copy-start | bytes 491524
  252.6 53.9 %collective-permute-start.1 = (bf16[160,2048]{1,0:T(8,128)(2,1)}, bf16[160,2048]{1,0:T(8,128)(2,1)}, u32[]{:S(2)}, u32[]{:S(2)}) collective-permute-start(bf16[160,2048]{1,0:T(8,128)(2,1)} %pad_maximum_fusion.2), channel_id=1, source_target_pairs={{0,8},{8,0},{4,12},{12,4},{16,24},{24,16},{20,28},{28,20},{32,40},... | collective-permute-start | bytes 1966088 | tf_op jit(solution)/shard_map/ppermute | solution.py:41
  257.1 3.5 copy-start.1
  260.2 4.6 %copy-start = (bf16[128,5120]{1,0:T(8,128)(2,1)}, bf16[128,5120]{1,0:T(8,128)(2,1)S(1)}, u32[]{:S(2)}) copy-start(bf16[128,5120]{1,0:T(8,128)(2,1)S(1)} %constant_dynamic-update-slice_fusion) | copy-start | bytes 3932164
  260.6 5.0 %copy-start.16 = (f32[128]{0:T(128)}, f32[128]{0:T(128)S(1)}, u32[]{:S(2)}) copy-start(f32[128]{0:T(128)S(1)} %add_rsqrt_fusion) | copy-start | bytes 1540
  261.4 4.2 %copy-start.7 = (f32[128,40]{0,1:T(8,128)S(1)}, f32[128,40]{0,1:T(8,128)}, u32[]{:S(2)}) copy-start(f32[128,40]{0,1:T(8,128)} %get-tuple-element.305) | copy-start | bytes 61444
  261.4 4.2 %copy-start.9 = (f32[128,40]{0,1:T(8,128)S(1)}, f32[128,40]{0,1:T(8,128)}, u32[]{:S(2)}) copy-start(f32[128,40]{0,1:T(8,128)} %get-tuple-element.306) | copy-start | bytes 61444
  261.5 9.0 %collective-permute-start.9 = (bf16[128,160]{0,1:T(8,128)(2,1)S(1)}, bf16[128,160]{0,1:T(8,128)(2,1)S(1)}, u32[]{:S(2)}, u32[]{:S(2)}) collective-permute-start(bf16[128,160]{0,1:T(8,128)(2,1)S(1)} %convolution_convert_fusion.1), channel_id=1, source_target_pairs={{0,4},{4,0},{8,12},{12,8},{16,20},{20,16},{24,28},{28,24},{32,36},... | collective-permute-start | bytes 122888 | tf_op jit(solution)/shard_map/ppermute | solution.py:41
  265.6 4.8 %collective-permute-start.7 = (bf16[128,160]{0,1:T(8,128)(2,1)S(1)}, bf16[128,160]{0,1:T(8,128)(2,1)S(1)}, u32[]{:S(2)}, u32[]{:S(2)}) collective-permute-start(bf16[128,160]{0,1:T(8,128)(2,1)S(1)} %bitcast.127), channel_id=1, source_target_pairs={{0,4},{4,0},{8,12},{12,8},{16,20},{20,16},{24,28},{28,24},{32,36},... | collective-permute-start | bytes 122888 | tf_op jit(solution)/shard_map/ppermute | solution.py:41
  268.5 40.5 %collective-permute-start.6 = (bf16[160,2048]{1,0:T(8,128)(2,1)}, bf16[160,2048]{1,0:T(8,128)(2,1)}, u32[]{:S(2)}, u32[]{:S(2)}) collective-permute-start(bf16[160,2048]{1,0:T(8,128)(2,1)} %pad_maximum_fusion.3), channel_id=1, source_target_pairs={{0,8},{8,0},{4,12},{12,4},{16,24},{24,16},{20,28},{28,20},{32,40},... | collective-permute-start | bytes 1966088 | tf_op jit(solution)/shard_map/ppermute | solution.py:41
  270.5 18.8 %collective-permute-start.10 = (bf16[256,160]{0,1:T(8,128)(2,1)S(1)}, bf16[256,160]{0,1:T(8,128)(2,1)S(1)}, u32[]{:S(2)}, u32[]{:S(2)}) collective-permute-start(bf16[256,160]{0,1:T(8,128)(2,1)S(1)} %pad_maximum_fusion.8), channel_id=1, source_target_pairs={{0,8},{8,0},{4,12},{12,4},{16,24},{24,16},{20,28},{28,20},{32,40},... | collective-permute-start | bytes 245768 | tf_op jit(solution)/shard_map/ppermute | solution.py:41
  273.9 17.3 %copy-start.13 = (s32[1024]{0:T(1024)S(1)}, s32[1024]{0:T(1024)}, u32[]{:S(2)}) copy-start(s32[1024]{0:T(1024)} %fusion.54) | copy-start | bytes 12292
  273.9 17.0 %collective-permute-start.8 = (bf16[256,160]{0,1:T(8,128)(2,1)S(1)}, bf16[256,160]{0,1:T(8,128)(2,1)S(1)}, u32[]{:S(2)}, u32[]{:S(2)}) collective-permute-start(bf16[256,160]{0,1:T(8,128)(2,1)S(1)} %pad_maximum_fusion.7), channel_id=1, source_target_pairs={{0,8},{8,0},{4,12},{12,4},{16,24},{24,16},{20,28},{28,20},{32,40},... | collective-permute-start | bytes 245768 | tf_op jit(solution)/shard_map/ppermute | solution.py:41
  296.1 5.0 %copy-start.2 = (bf16[160,1024]{0,1:T(8,128)(2,1)S(1)}, bf16[160,1024]{0,1:T(8,128)(2,1)}, u32[]{:S(2)}) copy-start(bf16[160,1024]{0,1:T(8,128)(2,1)} %copy.41) | copy-start | bytes 983044
  296.1 5.0 %copy-start.3 = (bf16[160,1024]{0,1:T(8,128)(2,1)S(1)}, bf16[160,1024]{0,1:T(8,128)(2,1)}, u32[]{:S(2)}) copy-start(bf16[160,1024]{0,1:T(8,128)(2,1)} %copy.39) | copy-start | bytes 983044
  296.1 5.0 %copy-start.18 = (pred[1024]{0:T(1024)(128)(4,1)S(1)}, pred[1024]{0:T(1024)(128)(4,1)}, u32[]{:S(2)}) copy-start(pred[1024]{0:T(1024)(128)(4,1)} %get-tuple-element.313) | copy-start | bytes 3076
  296.1 5.0 %copy-start.19 = (pred[1024]{0:T(1024)(128)(4,1)S(1)}, pred[1024]{0:T(1024)(128)(4,1)}, u32[]{:S(2)}) copy-start(pred[1024]{0:T(1024)(128)(4,1)} %get-tuple-element.314) | copy-start | bytes 3076
  311.6 4.7 %copy-start.17 = (f32[128]{0:T(128)S(1)}, f32[128]{0:T(128)}, u32[]{:S(2)}) copy-start(f32[128]{0:T(128)} %copy-done.16) | copy-start | bytes 1540
  316.3 2.8 copy-start.8
  316.3 2.8 copy-start.10
  316.3 2.9 copy-start.12
  319.2 50.6 %copy-start.6 = (pred[128,512]{0,1:T(8,128)(4,1)S(1)}, pred[128,512]{0,1:T(8,128)(4,1)}, u32[]{:S(2)}) copy-start(pred[128,512]{0,1:T(8,128)(4,1)} %fusion.38) | copy-start | bytes 196612
  322.4 1.0 copy-start.22
  324.8 0.7 copy-start.23
  328.7 1.0 copy-start.22
  331.1 0.7 copy-start.23
  335.0 1.0 copy-start.22
  337.4 0.7 copy-start.23
  341.3 1.0 copy-start.22
  347.7 1.0 copy-start.22
  354.0 1.0 copy-start.22
  356.4 0.7 copy-start.23
  360.3 1.0 copy-start.22
  366.6 1.0 copy-start.22
  370.3 0.9 copy-start.11
  370.3 1.1 copy-start.24
  (4 other events, 3.0 us)
Sparse Core Ops, SparseCore 0:
  11.1 147.5 all-gather.6
  161.7 137.8 all-gather.8
